TPU v7x, 32 devices: a whole 2x2x4 slice. The times are simulated.
32 devices in a mesh: pb: 8 (over z, y), ka: 4 (over x, core).
Axes of the slice: x: 2, y: 2, z: 4, core: 2. Of those that a mesh axis runs over, the one named last changes fastest.
Arguments:
- pair_trunk: bfloat16 [384, 384, 128], P('pb', 'ka'), may hold values from -40 to 40
- token_ids: int32 [3, 384], replicated, may hold values from 0 to 422, as said below
- w_rel: bfloat16 [139, 128], replicated, may hold values from -3.5 to 3.5
- cat_gain: float32 [256], replicated, may hold values from 0.1 to 1.9
- w_in: bfloat16 [256, 128], replicated, may hold values from -0.375 to 0.375
- trans_gain: float32 [2, 128], replicated, may hold values from 0.1 to 1.9
- trans_ab: bfloat16 [2, 128, 512], replicated, may hold values from -0.5 to 0.5
- trans_out: bfloat16 [2, 256, 128], replicated, may hold values from -0.375 to 0.375
- bias_gain: float32 [128], replicated, may hold values from 0.1 to 1.9
- w_bias: bfloat16 [128, 16], replicated, may hold values from -1.5 to 1.5
- normed: bfloat16 [8, 384, 768], P(None, 'pb', 'ka'), may hold values from -12 to 12
- w_proj: bfloat16 [4, 768, 768], P(None, None, 'ka'), may hold values from -1 to 1
- output_weight: bfloat16 [768, 768], P('ka'), may hold values from -0.21875 to 0.21875
Outputs:
- pair_cond: bfloat16 [384, 384, 128], P('pb', 'ka')
- update: bfloat16 [8, 384, 768], P(None, 'pb', 'ka')
Inputs may be any that keep to these rules, and one draw needn't show every extreme that they name: `token_ids`: row 0 is a token's residue number, row 1 its chain number, row 2 its entity number. Chain numbers start at 0 and never fall along the tokens; residue numbers never fall within a chain; all tokens of a chain share one entity. The last token's residue number is 422.
All inputs are finite; a program needn't handle non-finite values.
Results may differ from a plain program's by a relative error of at most 0.015.
The roundings to bfloat16 on the way count: a program that leaves them out, or rounds other values in their place, can miss the bound.
Values may be sent and summed in bfloat16 or wider, within the bound.
A program may use at most 64 MiB of HBM per device.

v0:
```python
import math
import jax
import jax.numpy as jnp
from jax import lax
from jax.sharding import PartitionSpec as P

HD = 48
RMAX = 32
SMAX = 2
REL = 139
EPS = 1e-05


def layer_norm(values, scaling):
    average = jnp.mean(values, axis=-1, keepdims=True)
    centered = values - average
    spread = jnp.mean(centered * centered, axis=-1, keepdims=True)
    return centered * lax.rsqrt(spread + EPS) * scaling


def relative_onehot(query_token_ids, key_ids, query_pos, key_pos):
    query_res = query_token_ids[0][:, None]
    key_res = key_ids[0][None, :]
    query_chain = query_token_ids[1][:, None]
    key_chain = key_ids[1][None, :]
    query_entity = query_token_ids[2][:, None]
    key_ent = key_ids[2][None, :]
    same_chain = query_chain == key_chain
    same_res = same_chain & (query_res == key_res)
    same_entity = query_entity == key_ent
    res_bins = 2 * RMAX + 2
    res_bin = jnp.where(same_chain, jnp.clip(query_res - key_res + RMAX, 0, 2 * RMAX), 2 * RMAX + 1)
    token_offset_bin = jnp.where(
        same_res, jnp.clip(query_pos[:, None] - key_pos[None, :] + RMAX, 0, 2 * RMAX), 2 * RMAX + 1
    )
    chain_offset_bin = jnp.where(
        same_entity, jnp.clip(query_chain - key_chain + SMAX, 0, 2 * SMAX), 2 * SMAX + 1
    )
    columns = jnp.arange(REL, dtype=jnp.int32)
    onehot = (columns == res_bin[..., None]) | (columns == (res_bins + token_offset_bin)[..., None])
    onehot = onehot | (columns == (2 * res_bins + chain_offset_bin)[..., None])
    onehot = onehot | (columns == REL - 1) & same_entity[..., None]
    return onehot.astype(jnp.bfloat16)


def condition_block(
    trunk_blk, onehot, w_rel, cat_gain, w_in, trans_gain, trans_ab, trans_out, bias_gain, w_bias
):
    half = trans_out.shape[1]
    relative = jnp.einsum("rkf,fc->rkc", onehot, w_rel, preferred_element_type=jnp.float32)
    joined = jnp.concatenate([trunk_blk.astype(jnp.float32), relative], axis=-1)
    normal_in = layer_norm(joined, cat_gain).astype(jnp.bfloat16)
    pair_state = jnp.einsum("rkf,fc->rkc", normal_in, w_in, preferred_element_type=jnp.float32)
    for layer_idx in range(2):
        normal_tr = layer_norm(pair_state, trans_gain[layer_idx]).astype(jnp.bfloat16)
        gate_up = jnp.einsum(
            "rkc,cf->rkf", normal_tr, trans_ab[layer_idx], preferred_element_type=jnp.float32
        )
        hidden = (jax.nn.silu(gate_up[..., :half]) * gate_up[..., half:]).astype(jnp.bfloat16)
        pair_state = pair_state + jnp.einsum(
            "rkf,fc->rkc", hidden, trans_out[layer_idx], preferred_element_type=jnp.float32
        )
    normal_b = layer_norm(pair_state, bias_gain).astype(jnp.bfloat16)
    bias_blk = jnp.einsum(
        "rkc,ch->hrk", normal_b, w_bias, preferred_element_type=jnp.float32
    ).astype(jnp.bfloat16)
    return (pair_state.astype(jnp.bfloat16), bias_blk)


def soft_weights(logits):
    row_max = jnp.max(logits, axis=-1, keepdims=True)
    expweights = jnp.exp(logits - row_max)
    return (expweights / jnp.sum(expweights, axis=-1, keepdims=True)).astype(jnp.bfloat16)


def shards(
    pair_trunk,
    token_ids,
    w_rel,
    cat_gain,
    w_in,
    trans_gain,
    trans_ab,
    trans_out,
    bias_gain,
    w_bias,
    normed,
    w_proj,
    output_weight,
):
    q_rows = pair_trunk.shape[0]
    k_rows = pair_trunk.shape[1]
    q_start = lax.axis_index("pb") * q_rows
    k_start = lax.axis_index("ka") * k_rows
    key_ids = lax.dynamic_slice_in_dim(token_ids, k_start, k_rows, 1)
    key_pos = k_start + jnp.arange(k_rows, dtype=jnp.int32)
    row_blk = 8

    def one_block(block_idx):
        begin_at = block_idx * row_blk
        trunk_blk = lax.dynamic_slice_in_dim(pair_trunk, begin_at, row_blk, 0)
        query_token_ids = lax.dynamic_slice_in_dim(token_ids, q_start + begin_at, row_blk, 1)
        query_pos = q_start + begin_at + jnp.arange(row_blk, dtype=jnp.int32)
        onehot = relative_onehot(query_token_ids, key_ids, query_pos, key_pos)
        return condition_block(
            trunk_blk,
            onehot,
            w_rel,
            cat_gain,
            w_in,
            trans_gain,
            trans_ab,
            trans_out,
            bias_gain,
            w_bias,
        )

    pair_blocks, bias_blocks = lax.map(one_block, jnp.arange(q_rows // row_blk, dtype=jnp.int32))
    pair_cond = pair_blocks.reshape(q_rows, k_rows, pair_blocks.shape[-1])
    bias_tile = jnp.transpose(bias_blocks, (1, 0, 2, 3)).reshape(
        bias_blocks.shape[1], q_rows, k_rows
    )
    samples = normed.shape[0]
    feat_local = normed.shape[2]
    heads_local = feat_local // HD
    scale_factor = 1.0 / math.sqrt(HD)
    projected = jnp.einsum(
        "sqf,pfe->psqe",
        lax.all_gather(normed, "ka", axis=2, tiled=True),
        w_proj,
        preferred_element_type=jnp.float32,
    )
    queries = projected[0].astype(jnp.bfloat16).reshape(samples, q_rows, heads_local, HD)
    kv_local = jnp.transpose(
        jnp.stack([projected[1], projected[2]], axis=1).astype(jnp.bfloat16), (0, 1, 3, 2)
    )
    bias_rows = lax.all_to_all(bias_tile, "ka", split_axis=0, concat_axis=2, tiled=True)
    kv_all = lax.all_gather(kv_local, "pb", axis=3, tiled=True)
    keys_all = kv_all[:, 0].reshape(samples, heads_local, HD, kv_all.shape[3])
    values_all = kv_all[:, 1].reshape(samples, heads_local, HD, kv_all.shape[3])
    logits = (
        jnp.einsum("sqhd,shdk->shqk", queries, keys_all, preferred_element_type=jnp.float32)
        * scale_factor
    )
    logits = logits + bias_rows[None].astype(jnp.float32)
    weights = soft_weights(logits)
    attended = jnp.einsum(
        "shqk,shdk->sqhd", weights, values_all, preferred_element_type=jnp.float32
    )
    gated_result = (
        attended.reshape(samples, q_rows, feat_local) * jax.nn.sigmoid(projected[3])
    ).astype(jnp.bfloat16)
    flat_gated = gated_result.reshape(samples * q_rows, feat_local)
    summed = lax.psum_scatter(
        jnp.einsum(
            "fe,nf->en", output_weight, flat_gated, preferred_element_type=jnp.float32
        ).astype(jnp.bfloat16),
        "ka",
        scatter_dimension=0,
        tiled=True,
    ).astype(jnp.float32)
    update = jnp.transpose(summed).reshape(samples, q_rows, feat_local).astype(jnp.bfloat16)
    return (pair_cond, update)


def solution(mesh):
    in_specs = (
        P("pb", "ka", None),
        P(),
        P(),
        P(),
        P(),
        P(),
        P(),
        P(),
        P(),
        P(),
        P(None, "pb", "ka"),
        P(None, None, "ka"),
        P("ka", None),
    )
    out_specs = (P("pb", "ka", None), P(None, "pb", "ka"))
    return jax.shard_map(shards, mesh=mesh, in_specs=in_specs, out_specs=out_specs, check_vma=False)
```

profile of v0, /device:TPU:0, one launch (start us, length us, event | category | flops | bytes accessed | tf_op | source)
XLA Modules:
  0.0 148.7 jit_solution(9345763957200801556)
XLA Ops:
  7.2 1.3 copy.25
  8.5 14.3 %all_gather.6 = bf16[8,48,768]{1,0,2:T(8,128)(2,1)S(1)} all-gather(bf16[8,48,192]{1,0,2:T(8,128)(2,1)S(1)} %copy.25), channel_id=1, replica_groups=mesh['pb'=8,'ka'=4] {'ka'}, dimensions={2}, use_global_device_ids=true | all-gather | bytes 737280 | tf_op jit(solution)/shard_map/all_gather | solution.py:129
  22.8 1.6 %copy.26 = bf16[8,48,768]{2,1,0:T(8,128)(2,1)} copy(bf16[8,48,768]{1,0,2:T(8,128)(2,1)S(1)} %all_gather.6) | data formatting | bytes 1179648 | tf_op jit(solution)/shard_map/all_gather | solution.py:129
  24.5 1.8 %fusion.70 = (bf16[4,8,48,192]{3,2,1,0:T(8,128)(2,1)S(1)}, f32[4,8,48,192]{3,2,1,0:T(8,128)S(1)}) fusion(bf16[8,48,768]{2,1,0:T(8,128)(2,1)} %copy.26, bf16[4,768,192]{1,2,0:T(8,128)(2,1)S(1)} %copy-done), kind=kOutput, calls=%fused_computation.118 | convolution fusion | flops 453279744 | bytes 3538944 | tf_op jit(solution)/shard_map/sqf,pfe->psqe/dot_general | solution.py:127
  28.2 60.4 %while.13 = (s32[]{:T(128)}, bf16[6,8,96,128]{3,2,1,0:T(8,128)(2,1)}, bf16[6,16,8,96]{3,1,2,0:T(8,128)(2,1)}, s32[6]{0:T(128)S(1)}, bf16[48,96,128]{2,1,0:T(8,12...) while((s32[]{:T(128)}, ...), condition=%wide.region_10.11_spmd.clone, body=%wide.region_0.10_spmd.clone.sunk | while | flops 390749440 | bytes 15165903 | solution.py:118
  31.4 1.1 fusion.91
  35.6 1.0 bitcast_dynamic-update-slice_fusion.2
  41.5 1.1 fusion.91
  51.6 1.1 fusion.91
  61.6 1.1 fusion.91
  71.7 1.1 fusion.91
  81.8 1.1 fusion.91
  85.9 1.0 bitcast_dynamic-update-slice_fusion.2
  88.6 1.7 %copy.48 = bf16[16,6,8,96]{3,2,1,0:T(8,128)(2,1)} copy(bf16[16,6,8,96]{3,0,2,1:T(8,128)(2,1)} %bitcast.136) | data formatting | bytes 294912 | tf_op jit(solution)/shard_map/transpose | solution.py:120
  90.3 4.0 %all-to-all-start = ((bf16[16,48,96]{2,1,0:T(8,128)(2,1)}), bf16[16,48,96]{2,1,0:T(8,128)(2,1)}, u32[]{:S(2)}, u32[]{:S(2)}) async-start(bf16[16,48,96]{2,1,0:T(8,128)(2,1)} %bitcast.106), calls=%async_computation | async-start | bytes 393216 | tf_op jit(solution)/shard_map/all_to_all | solution.py:137
  96.3 3.3 %all-to-all-done = bf16[16,48,96]{2,1,0:T(8,128)(2,1)} async-done(((bf16[16,48,96]{2,1,0:T(8,128)(2,1)}), bf16[16,48,96]{2,1,0:T(8,128)(2,1)}, u32[]{:S(2)}, u32[]{:S(2)}) %all-to-all-start) | async-done | bytes 147488 | tf_op jit(solution)/shard_map/all_to_all | solution.py:137
  101.8 3.4 %fusion.68 = (bf16[8,1,192,384]{2,3,0,1:T(8,128)(2,1)S(1)}, bf16[8,1,192,384]{2,3,0,1:T(8,128)(2,1)}) fusion(bf16[8,2,192,384]{2,3,0,1:T(8,128)(2,1)} %all-gather.2.cloned.1.call-done), kind=kLoop, calls=%fused_computation.116 | loop fusion | bytes 4718592 | tf_op jit(solution)/shard_map/slice | solution.py:139
  105.1 2.5 %copy.27 = bf16[8,1,192,384]{3,2,0,1:T(8,128)(2,1)} copy(bf16[8,1,192,384]{2,3,0,1:T(8,128)(2,1)} %get-tuple-element.183) | data formatting | bytes 2359296 | tf_op jit(solution)/shard_map/slice | solution.py:140
  107.7 1.5 %copy.28 = bf16[8,1,192,384]{3,2,0,1:T(8,128)(2,1)} copy(bf16[8,1,192,384]{2,3,0,1:T(8,128)(2,1)S(1)} %get-tuple-element.182) | data formatting | bytes 2359296 | tf_op jit(solution)/shard_map/slice | solution.py:139
  109.2 3.6 %fusion.71 = (f32[8,4,48]{2,1,0:T(4,128)S(1)}, f32[8,4,48,384]{3,2,1,0:T(8,128)}) fusion(f32[4,48,384]{2,1,0:T(8,128)} %reshape.365, bf16[8,4,48,384]{3,2,1,0:T(8,128)(2,1)} %bitcast.135, bf16[8,48,4,48]{3,2,1,0:T(4,128)(2,1)S(1)} %copy-done.5), kind=kOutput, calls=%fused_computation.119 | convolution fusion | flops 58982784 | bytes 3987456 | tf_op jit(solution)/shard_map/sub | solution.py:72
  112.8 2.3 %convolution_bitcast_fusion.1 = f32[8,48,4,48]{1,3,2,0:T(8,128)S(1)} fusion(bf16[8,4,48,384]{3,2,1,0:T(8,128)(2,1)S(1)} %bitcast.134, f32[8,4,48,384]{3,2,1,0:T(8,128)} %get-tuple-element.190, f32[8,4,48]{2,1,0:T(4,128)S(1)} %get-tuple-element.189), kind=kOutput, calls=%fused_computation.93 | convolution fusion | flops 57802752 | bytes 3840000 | tf_op jit(solution)/shard_map/shqk,shdk->sqhd/dot_general | solution.py:147
  116.5 1.1 copy.35
  117.6 22.5 %reduce-scatter.4.cloned.1.call-done = bf16[192,384]{1,0:T(8,128)(2,1)} async-done(((bf16[768,384]{1,0:T(8,128)(2,1)}), bf16[192,384]{1,0:T(8,128)(2,1)}) %reduce-scatter.4.cloned.1.call-update) | async-done | bytes 147472
  140.1 1.7 %copy.36 = bf16[192,384]{0,1:T(8,128)(2,1)} copy(bf16[192,384]{1,0:T(8,128)(2,1)} %reduce-scatter.4.cloned.1.call-done) | data formatting | bytes 294912
  (244 shorter events, 54.6 us)
Async XLA Ops:
  7.2 17.3 %copy-start = (bf16[4,768,192]{1,2,0:T(8,128)(2,1)S(1)}, bf16[4,768,192]{1,2,0:T(8,128)(2,1)}, u32[]{:S(2)}) copy-start(bf16[4,768,192]{1,2,0:T(8,128)(2,1)} %param.26) | copy-start | bytes 3538948
  7.2 94.6 %all-gather.2.cloned.1.call-start = ((), (), s32[]{:S(2)}) async-start(), calls=%async_computation.2 | async-start | bytes 3538944 | tf_op jit(solution)/shard_map/all_gather | solution.py:138
  26.3 1.7 %copy-start.9 = (s32[3,384]{1,0:T(4,128)S(1)}, s32[3,384]{1,0:T(4,128)}, u32[]{:S(2)}) copy-start(s32[3,384]{1,0:T(4,128)} %param.16) | copy-start | bytes 13828
  26.3 1.8 %copy-start.1 = (bf16[2,128,512]{2,1,0:T(8,128)(2,1)S(1)}, bf16[2,128,512]{2,1,0:T(8,128)(2,1)}, u32[]{:S(2)}) copy-start(bf16[2,128,512]{2,1,0:T(8,128)(2,1)} %param.21) | copy-start | bytes 786436
  26.4 1.8 %copy-start.7 = (bf16[128,16]{0,1:T(8,128)(2,1)S(1)}, bf16[128,16]{0,1:T(8,128)(2,1)}, u32[]{:S(2)}) copy-start(bf16[128,16]{0,1:T(8,128)(2,1)} %param.24) | copy-start | bytes 12292
  26.4 1.8 %copy-start.8 = (f32[2,128]{1,0:T(2,128)S(1)}, f32[2,128]{1,0:T(2,128)}, u32[]{:S(2)}) copy-start(f32[2,128]{1,0:T(2,128)} %param.20) | copy-start | bytes 3076
  26.4 1.7 %copy-start.10 = (f32[128]{0:T(128)S(1)}, f32[128]{0:T(128)}, u32[]{:S(2)}) copy-start(f32[128]{0:T(128)} %param.23) | copy-start | bytes 1540
  26.4 1.7 %copy-start.12 = (bf16[256,128]{1,0:T(8,128)(2,1)S(1)}, bf16[256,128]{1,0:T(8,128)(2,1)}, u32[]{:S(2)}) copy-start(bf16[256,128]{1,0:T(8,128)(2,1)} %param.19) | copy-start | bytes 196612
  26.4 1.7 %copy-start.13 = (bf16[139,128]{1,0:T(8,128)(2,1)S(1)}, bf16[139,128]{1,0:T(8,128)(2,1)}, u32[]{:S(2)}) copy-start(bf16[139,128]{1,0:T(8,128)(2,1)} %param.17) | copy-start | bytes 106756
  26.4 1.7 %copy-start.14 = (f32[256]{0:T(256)S(1)}, f32[256]{0:T(256)}, u32[]{:S(2)}) copy-start(f32[256]{0:T(256)} %param.18) | copy-start | bytes 3076
  33.5 0.9 copy-start.11
  43.5 0.9 copy-start.11
  53.6 0.9 copy-start.11
  63.7 0.9 copy-start.11
  73.7 0.9 copy-start.11
  83.8 0.9 copy-start.11
  88.6 5.9 %copy-start.4 = (bf16[1,8,48,192]{3,2,1,0:T(8,128)(2,1)S(1)}, bf16[1,8,48,192]{3,2,1,0:T(8,128)(2,1)}, u32[]{:S(2)}) copy-start(bf16[1,8,48,192]{3,2,1,0:T(8,128)(2,1)} %get-tuple-element.184) | copy-start | bytes 442372
  90.3 9.4 %all-to-all-start = ((bf16[16,48,96]{2,1,0:T(8,128)(2,1)}), bf16[16,48,96]{2,1,0:T(8,128)(2,1)}, u32[]{:S(2)}, u32[]{:S(2)}) async-start(bf16[16,48,96]{2,1,0:T(8,128)(2,1)} %bitcast.106), calls=%async_computation | async-start | bytes 393216 | tf_op jit(solution)/shard_map/all_to_all | solution.py:137
  94.3 45.9 %reduce-scatter.4.cloned.1.call-start = ((), (), s32[]{:S(2)}) async-start(), calls=%async_computation.3 | async-start | bytes 737280
  107.7 1.5 %copy-start.5 = (bf16[8,48,4,48]{3,2,1,0:T(4,128)(2,1)S(1)}, bf16[8,48,4,48]{3,2,1,0:T(4,128)(2,1)}, u32[]{:S(2)}) copy-start(bf16[8,48,4,48]{3,2,1,0:T(4,128)(2,1)} %convert_element_type.75) | copy-start | bytes 442372
  109.2 3.7 %copy-start.2 = (bf16[8,1,192,384]{3,2,0,1:T(8,128)(2,1)S(1)}, bf16[8,1,192,384]{3,2,0,1:T(8,128)(2,1)}, u32[]{:S(2)}) copy-start(bf16[8,1,192,384]{3,2,0,1:T(8,128)(2,1)} %copy.27) | copy-start | bytes 3538948
  115.1 1.0 copy-start.3
  115.1 1.1 copy-start.6
Sparse Core Ops, SparseCore 0:
  28.1 60.9 all-gather.1
  117.7 22.3 reduce-scatter.3
where the time goes:
time: 150 us; the launch traced here: 149 us
  matrix products  36 us (24%)
  waiting for transfers between devices  25.9 us (17%)
  other arithmetic  24.9 us (17%)
  local copies, waits for them, and re-layouts  24.6 us (16%)
  blocking collectives  14.3 us (10%)
  between operations  14.3 us (10%)
  loops' own time  4.55 us (3%)
  starting transfers between devices  4.06 us (3%)
    unnamed x3, waiting for transfers between devices  22.6 us
    all_gather x1, blocking collectives, shards(): lax.all_gather(normed, 'ka', axis=2, tiled=True)  14.3 us
    dot_general x12, matrix products, condition_block(): jnp.einsum('rkf,fc->rkc', hidden, trans_out[layer_idx], preferred_element...  8.85 us
    reduce_sum x24, other arithmetic, layer_norm(): spread = jnp.mean(centered * centered, axis=-1, keepdims=True)  8.37 us
    reduce_sum x12, other arithmetic, layer_norm(): average = jnp.mean(values, axis=-1, keepdims=True)  7.67 us
    dot_general x6, matrix products, condition_block(): jnp.einsum('rkc,ch->hrk', normal_b, w_bias, preferred_element_type=jnp.fl...  6.08 us
    convert_element_type x6, other arithmetic, condition_block(): joined = jnp.concatenate([trunk_blk.astype(jnp.float32), relative], axis=-1)  5.75 us
    dot_general x12, matrix products, condition_block(): jnp.einsum('rkc,cf->rkf', normal_tr, trans_ab[layer_idx], preferred_eleme...  5.08 us
  transfers between devices with their start and end apart: 3, of which 2 were waited for; matrix products, arithmetic and copies ran while one was open for 41% of the time, Pallas kernels for 0%

commit v1 on v0

--- a/solution.py
+++ b/solution.py
@@ -124,12 +124,38 @@
     feat_local = normed.shape[2]
     heads_local = feat_local // HD
     scale_factor = 1.0 / math.sqrt(HD)
-    projected = jnp.einsum(
+    size, mine, rows = (lax.axis_size("ka"), lax.axis_index("ka"), normed.shape[2])
+    upward = [(i, (i + 1) % size) for i in range(size)]
+    left = [(i, (i - 1) % size) for i in range(size)]
+    half_2 = size // 2
+    from_left = from_right = normed
+    total = jnp.einsum(
         "sqf,pfe->psqe",
-        lax.all_gather(normed, "ka", axis=2, tiled=True),
-        w_proj,
+        normed,
+        lax.dynamic_slice_in_dim(w_proj, mine * rows, normed.shape[2], axis=1),
         preferred_element_type=jnp.float32,
     )
+    for lap in range(1, half_2 + 1):
+        from_left = lax.ppermute(from_left, "ka", upward)
+        if lap < size - half_2:
+            from_right = lax.ppermute(from_right, "ka", left)
+            total = total + jnp.einsum(
+                "sqf,pfe->psqe",
+                from_right,
+                lax.dynamic_slice_in_dim(
+                    w_proj, (mine + lap) % size * rows, from_right.shape[2], axis=1
+                ),
+                preferred_element_type=jnp.float32,
+            )
+        total = total + jnp.einsum(
+            "sqf,pfe->psqe",
+            from_left,
+            lax.dynamic_slice_in_dim(
+                w_proj, (mine - lap) % size * rows, from_left.shape[2], axis=1
+            ),
+            preferred_element_type=jnp.float32,
+        )
+    projected = total
     queries = projected[0].astype(jnp.bfloat16).reshape(samples, q_rows, heads_local, HD)
     kv_local = jnp.transpose(
         jnp.stack([projected[1], projected[2]], axis=1).astype(jnp.bfloat16), (0, 1, 3, 2)

time: 150 us -> 138 us (0.920)
  local copies, waits for them, and re-layouts: 24.6 us -> 17.2 us
  blocking collectives: 14.3 us -> 10.7 us
    all_gather x1 -> x0, blocking collectives: 14.3 us -> none  [shards(): lax.all_gather(normed, 'ka', axis=2, tiled=True)]
    all_to_all x0 -> x1, blocking collectives: none -> 10.7 us  [shards(): lax.all_to_all(bias_tile, 'ka', split_axis=0, concat_axis=2, tiled=True)]
    ppermute x0 -> x3, starting transfers between devices: none -> 4.59 us  [the longest x2 2.61 us: shards(): from_left = lax.ppermute(from_left, 'ka', upward)]
    all_to_all x1 -> x0, starting transfers between devices: 3.99 us -> none  [shards(): lax.all_to_all(bias_tile, 'ka', split_axis=0, concat_axis=2, tiled=True)]
    ppermute x0 -> x3, waiting for transfers between devices: none -> 3.97 us  [the longest x2 3.97 us: shards(): from_left = lax.ppermute(from_left, 'ka', upward)]
    dot_general x6, matrix products: 6.08 us -> 2.41 us  [condition_block(): jnp.einsum('rkc,ch->hrk', normal_b, w_bias, preferred_element_type=jnp.fl...]
    all_to_all x1 -> x0, waiting for transfers between devices: 3.34 us -> none  [shards(): lax.all_to_all(bias_tile, 'ka', split_axis=0, concat_axis=2, tiled=True)]
    dot_general x1 -> x4, matrix products: 1.85 us -> 4.06 us  [the longest x2 2.16 us: shards(): jnp.einsum('sqf,pfe->psqe', from_left, lax.dynamic_slice_in_dim(w_proj, (...]
  transfers between devices with their start and end apart: 3 -> 5, of which waited for: 2 -> 3; matrix products, arithmetic and copies ran while one was open for 41% -> 41% of each run, Pallas kernels for 0% -> 0%
where the time goes in v1:
time: 138 us; the launch traced here: 137 us
  matrix products  34.6 us (25%)
  waiting for transfers between devices  25.8 us (19%)
  other arithmetic  25 us (18%)
  local copies, waits for them, and re-layouts  17.2 us (12%)
  between operations  14.4 us (10%)
  blocking collectives  10.7 us (8%)
  loops' own time  5 us (4%)
  starting transfers between devices  4.67 us (3%)
    unnamed x3, waiting for transfers between devices  21.8 us
    all_to_all x1, blocking collectives, shards(): lax.all_to_all(bias_tile, 'ka', split_axis=0, concat_axis=2, tiled=True)  10.7 us
    dot_general x12, matrix products, condition_block(): jnp.einsum('rkf,fc->rkc', hidden, trans_out[layer_idx], preferred_element...  8.82 us
    reduce_sum x24, other arithmetic, layer_norm(): spread = jnp.mean(centered * centered, axis=-1, keepdims=True)  8.34 us
    reduce_sum x12, other arithmetic, layer_norm(): average = jnp.mean(values, axis=-1, keepdims=True)  7.67 us
    convert_element_type x6, other arithmetic, condition_block(): joined = jnp.concatenate([trunk_blk.astype(jnp.float32), relative], axis=-1)  5.79 us
    dot_general x12, matrix products, condition_block(): jnp.einsum('rkc,cf->rkf', normal_tr, trans_ab[layer_idx], preferred_eleme...  5.08 us
    another operation x1, loops' own time, shards(): lax.map(one_block, jnp.arange(q_rows // row_blk, dtype=jnp.int32))  5 us
  transfers between devices with their start and end apart: 5, of which 3 were waited for; matrix products, arithmetic and copies ran while one was open for 41% of the time, Pallas kernels for 0%

profile of v1, /device:TPU:0, one launch (start us, length us, event | category | flops | bytes accessed | tf_op | source)
XLA Modules:
  0.0 137.3 jit_solution(17144196762787633392)
XLA Ops:
  7.8 2.0 %collective-permute-start = (bf16[8,48,192]{2,1,0:T(8,128)(2,1)}, bf16[8,48,192]{2,1,0:T(8,128)(2,1)S(1)}, u32[]{:S(2)}, u32[]{:S(2)}) collective-permute-start(bf16[8,48,192]{2,1,0:T(8,128)(2,1)} %param.25), channel_id=1, source_target_pairs={{0,3},{1,0},{2,1},{3,2},{4,7},{5,4},{6,5},{7,6},{8,11},{9,8},{10,9... | collective-permute-start | bytes 442376 | tf_op jit(solution)/shard_map/ppermute | solution.py:141
  9.8 1.4 %fusion.59 = f32[4,192,8,48]{1,3,2,0:T(8,128)S(1)} fusion(bf16[4,768,192]{1,2,0:T(8,128)(2,1)S(1)} %copy-done, s32[]{:T(128)S(6)} %select_n.59, bf16[8,48,192]{2,1,0:T(8,128)(2,1)} %param.25), kind=kOutput, calls=%fused_computation.107 | convolution fusion | flops 113246208 | bytes 1720324 | tf_op jit(solution)/shard_map/sqf,pfe->psqe/dot_general | solution.py:132
  11.4 1.9 %collective-permute-done.1 = bf16[8,48,192]{2,1,0:T(8,128)(2,1)S(1)} collective-permute-done((bf16[8,48,192]{2,1,0:T(8,128)(2,1)}, bf16[8,48,192]{2,1,0:T(8,128)(2,1)S(1)}, u32[]{:S(2)}, u32[]{:S(2)}) %collective-permute-start.1) | collective-permute-done | bytes 147488 | tf_op jit(solution)/shard_map/ppermute | solution.py:139
  13.3 2.1 %collective-permute-start.2 = (bf16[8,48,192]{2,1,0:T(8,128)(2,1)S(1)}, bf16[8,48,192]{2,1,0:T(8,128)(2,1)S(1)}, u32[]{:S(2)}, u32[]{:S(2)}) collective-permute-start(bf16[8,48,192]{2,1,0:T(8,128)(2,1)S(1)} %collective-permute-done.1), channel_id=1, source_target_pairs={{0,1},{1,2},{2,3},{3,0},{4,5},{5,6},{6,7},{7,4},{8,9},{9,10},{10,1... | collective-permute-start | bytes 442376 | tf_op jit(solution)/shard_map/ppermute | solution.py:139
  16.3 2.1 %collective-permute-done.2 = bf16[8,48,192]{2,1,0:T(8,128)(2,1)S(1)} collective-permute-done((bf16[8,48,192]{2,1,0:T(8,128)(2,1)S(1)}, bf16[8,48,192]{2,1,0:T(8,128)(2,1)S(1)}, u32[]{:S(2)}, u32[]{:S(2)}) %collective-permute-start.2) | collective-permute-done | bytes 147488 | tf_op jit(solution)/shard_map/ppermute | solution.py:139
  18.4 1.7 %fusion.87 = (bf16[4,8,48,192]{3,2,1,0:T(8,128)(2,1)S(1)}, f32[4,8,48,192]{3,2,1,0:T(8,128)}) fusion(bf16[8,48,192]{2,1,0:T(8,128)(2,1)S(1)} %collective-permute-done.2, bf16[4,768,192]{1,2,0:T(8,128)(2,1)S(1)} %copy-done, s32[]{:T(128)S(6)} %select_n.65, f32[4,192,8,48]{1,3,2,0:T(8,128)S(1)} %fusion.55, f32[4,192,8,48]{1,3,2,0:T(8,128)S(1)} %fusion.59, ...), kind=kOutput, calls=%fused_computation.135 | convolution fusion | flops 114425856 | bytes 7077892 | tf_op jit(solution)/shard_map/sqf,pfe->psqe/dot_general | solution.py:150
  21.2 56.7 %while.13 = (s32[]{:T(128)}, bf16[6,8,96,128]{3,2,1,0:T(8,128)(2,1)}, bf16[6,16,8,96]{3,1,2,0:T(8,128)(2,1)S(1)}, s32[6]{0:T(128)S(1)}, bf16[48,96,128]{2,1,0:T(...) while((s32[]{:T(128)}, ...), condition=%wide.region_10.11_spmd.clone, body=%wide.region_0.10_spmd.clone.sunk | while | flops 390749440 | bytes 14643635 | solution.py:118
  24.5 1.1 fusion.108
  28.6 1.0 bitcast_dynamic-update-slice_fusion.2
  34.0 1.1 fusion.108
  43.4 1.1 fusion.108
  52.9 1.1 fusion.108
  62.3 1.1 fusion.108
  71.8 1.1 fusion.108
  77.9 10.7 %all_to_all.4 = bf16[16,48,96]{2,1,0:T(8,128)(2,1)S(1)} all-to-all(bf16[16,48,96]{2,1,0:T(8,128)(2,1)S(1)} %bitcast.164), channel_id=1, replica_groups=mesh['pb'=8,'ka'=4] {'ka'}, dimensions={0} | all-to-all | bytes 294912 | tf_op jit(solution)/shard_map/all_to_all | solution.py:163
  90.1 1.1 fusion.53
  91.4 3.3 %fusion.85 = (bf16[8,1,192,384]{2,3,0,1:T(8,128)(2,1)S(1)}, bf16[8,1,192,384]{2,3,0,1:T(8,128)(2,1)}) fusion(bf16[8,2,192,384]{2,3,0,1:T(8,128)(2,1)} %all-gather.2.cloned.1.call-done), kind=kLoop, calls=%fused_computation.133 | loop fusion | bytes 4718592 | tf_op jit(solution)/shard_map/slice | solution.py:165
  94.6 2.5 %copy.37 = bf16[8,1,192,384]{3,2,0,1:T(8,128)(2,1)} copy(bf16[8,1,192,384]{2,3,0,1:T(8,128)(2,1)} %get-tuple-element.183) | data formatting | bytes 2359296 | tf_op jit(solution)/shard_map/slice | solution.py:166
  97.1 1.5 %copy.38 = bf16[8,1,192,384]{3,2,0,1:T(8,128)(2,1)} copy(bf16[8,1,192,384]{2,3,0,1:T(8,128)(2,1)S(1)} %get-tuple-element.182) | data formatting | bytes 2359296 | tf_op jit(solution)/shard_map/slice | solution.py:165
  98.6 3.7 %fusion.88 = (f32[8,4,48]{2,1,0:T(4,128)S(1)}, f32[8,4,48,384]{3,2,1,0:T(8,128)}) fusion(f32[4,48,384]{2,1,0:T(8,128)} %reshape.365, bf16[8,4,48,384]{3,2,1,0:T(8,128)(2,1)} %bitcast.163, bf16[8,48,4,48]{3,2,1,0:T(4,128)(2,1)S(1)} %convert_element_type.75), kind=kOutput, calls=%fused_computation.136 | convolution fusion | flops 58982784 | bytes 3987456 | tf_op jit(solution)/shard_map/sub | solution.py:72
  102.3 2.3 %convolution_bitcast_fusion = f32[8,48,4,48]{1,3,2,0:T(8,128)S(1)} fusion(bf16[8,4,48,384]{3,2,1,0:T(8,128)(2,1)S(1)} %bitcast.162, f32[8,4,48,384]{3,2,1,0:T(8,128)} %get-tuple-element.190, f32[8,4,48]{2,1,0:T(4,128)S(1)} %get-tuple-element.189), kind=kOutput, calls=%fused_computation.93 | convolution fusion | flops 57802752 | bytes 3840000 | tf_op jit(solution)/shard_map/shqk,shdk->sqhd/dot_general | solution.py:173
  106.0 1.0 copy.48
  107.0 21.7 %reduce-scatter.4.cloned.1.call-done = bf16[192,384]{1,0:T(8,128)(2,1)} async-done(((bf16[768,384]{1,0:T(8,128)(2,1)}), bf16[192,384]{1,0:T(8,128)(2,1)}) %reduce-scatter.4.cloned.1.call-update) | async-done | bytes 147472
  128.8 1.7 %copy.49 = bf16[192,384]{0,1:T(8,128)(2,1)} copy(bf16[192,384]{1,0:T(8,128)(2,1)} %reduce-scatter.4.cloned.1.call-done) | data formatting | bytes 294912
  (233 shorter events, 49.8 us)
Async XLA Ops:
  7.2 2.6 %copy-start = (bf16[4,768,192]{1,2,0:T(8,128)(2,1)S(1)}, bf16[4,768,192]{1,2,0:T(8,128)(2,1)}, u32[]{:S(2)}) copy-start(bf16[4,768,192]{1,2,0:T(8,128)(2,1)} %param.26) | copy-start | bytes 3538948
  7.2 4.1 %copy-start.6 = (s32[3,384]{1,0:T(4,128)S(1)}, s32[3,384]{1,0:T(4,128)}, u32[]{:S(2)}) copy-start(s32[3,384]{1,0:T(4,128)} %param.16) | copy-start | bytes 13828
  7.2 84.2 %all-gather.2.cloned.1.call-start = ((), (), s32[]{:S(2)}) async-start(), calls=%async_computation.2 | async-start | bytes 3538944 | tf_op jit(solution)/shard_map/all_gather | solution.py:164
  7.2 6.0 %collective-permute-start.1 = (bf16[8,48,192]{2,1,0:T(8,128)(2,1)}, bf16[8,48,192]{2,1,0:T(8,128)(2,1)S(1)}, u32[]{:S(2)}, u32[]{:S(2)}) collective-permute-start(bf16[8,48,192]{2,1,0:T(8,128)(2,1)} %param.25), channel_id=1, source_target_pairs={{0,1},{1,2},{2,3},{3,0},{4,5},{5,6},{6,7},{7,4},{8,9},{9,10},{10,1... | collective-permute-start | bytes 442376 | tf_op jit(solution)/shard_map/ppermute | solution.py:139
  7.8 8.0 %collective-permute-start = (bf16[8,48,192]{2,1,0:T(8,128)(2,1)}, bf16[8,48,192]{2,1,0:T(8,128)(2,1)S(1)}, u32[]{:S(2)}, u32[]{:S(2)}) collective-permute-start(bf16[8,48,192]{2,1,0:T(8,128)(2,1)} %param.25), channel_id=1, source_target_pairs={{0,3},{1,0},{2,1},{3,2},{4,7},{5,4},{6,5},{7,6},{8,11},{9,8},{10,9... | collective-permute-start | bytes 442376 | tf_op jit(solution)/shard_map/ppermute | solution.py:141
  13.3 5.1 %collective-permute-start.2 = (bf16[8,48,192]{2,1,0:T(8,128)(2,1)S(1)}, bf16[8,48,192]{2,1,0:T(8,128)(2,1)S(1)}, u32[]{:S(2)}, u32[]{:S(2)}) collective-permute-start(bf16[8,48,192]{2,1,0:T(8,128)(2,1)S(1)} %collective-permute-done.1), channel_id=1, source_target_pairs={{0,1},{1,2},{2,3},{3,0},{4,5},{5,6},{6,7},{7,4},{8,9},{9,10},{10,1... | collective-permute-start | bytes 442376 | tf_op jit(solution)/shard_map/ppermute | solution.py:139
  20.0 1.0 copy-start.1
  20.1 1.0 copy-start.4
  20.1 1.0 copy-start.5
  20.1 1.1 copy-start.7
  20.1 1.1 copy-start.8
  20.1 1.1 copy-start.9
  20.1 1.1 copy-start.10
  20.1 1.1 copy-start.11
  21.0 107.8 %reduce-scatter.4.cloned.1.call-start = ((), (), s32[]{:S(2)}) async-start(), calls=%async_computation.3 | async-start | bytes 737280
  98.6 3.7 %copy-start.2 = (bf16[8,1,192,384]{3,2,0,1:T(8,128)(2,1)S(1)}, bf16[8,1,192,384]{3,2,0,1:T(8,128)(2,1)}, u32[]{:S(2)}) copy-start(bf16[8,1,192,384]{3,2,0,1:T(8,128)(2,1)} %copy.37) | copy-start | bytes 3538948
  104.6 1.0 copy-start.3
Sparse Core Ops, SparseCore 0:
  21.1 63.4 all-gather.1
  107.2 21.5 reduce-scatter.3
